TPU v7x, 128 devices: a whole 4x4x4 slice. The times are simulated.
128 devices in a mesh: front: 4 (over y), rows: 32 (over z, x, core).
Axes of the slice: x: 4, y: 4, z: 4, core: 2. Of those that a mesh axis runs over, the one named last changes fastest.
Arguments:
- panel_g: bfloat16 [4, 32, 2048, 256], P('front', 'rows'), may hold values from -6 to 6
- refl_root: bfloat16 [4, 32, 2048, 512], P('front', 'rows'), may hold values from -6 to 6
- refl_mid: bfloat16 [4, 32, 4096, 512], P('front', 'rows'), may hold values from -6 to 6
- refl_leaf: bfloat16 [4, 32, 4096, 512], P('front', 'rows'), may hold values from -6 to 6
- tri_root: float32 [512, 512], replicated, as said below
- tri_mid: float32 [4, 512, 512], P('front'), as said below
- tri_leaf: float32 [4, 512, 512], P('front'), as said below
- route_root: int32 [4, 32, 16], P('front', 'rows'), may hold values from 0 to 3, as said below
- route_mid: int32 [4, 32, 32], P('front', 'rows'), may hold values from 0 to 3, as said below
Outputs:
- leaf_g: bfloat16 [4, 32, 4096, 256], P('front', 'rows')
Inputs may be any that keep to these rules, and one draw needn't show every extreme that they name: `route_root`: on every device at most 8 blocks name the same front, and some front is named by exactly 8 of them. `route_mid`: on every device each front is named by exactly 8 slots. `tri_root`: upper triangular. `tri_mid`: upper triangular. `tri_leaf`: upper triangular.
All inputs are finite; a program needn't handle non-finite values.
Results may differ from a plain program's by a relative error of at most 0.01.
Values may be sent and summed in bfloat16 or wider, within the bound.
No kernel may reach another device: no remote copies, remote signals or barrier semaphores. Data moves between devices by JAX's collectives and lax.ppermute only.
A program may use at most 64 MiB of HBM per device.

v0:
```python
import jax
import jax.numpy as jnp
from jax import lax
from jax.experimental import pallas as pl
from jax.experimental.pallas import tpu as pltpu
from jax.sharding import Mesh
from jax.sharding import PartitionSpec as P


BLOCK = 128
FRONTS = 4
CAP = 8
COLS = 256
REFL = 512
CHUNK = CAP * BLOCK
FLAGS = 16
TILE = 512
ROWS = ("rows_0", "rows_1", "rows_2")
ALL = ("front",) + ROWS
F32 = jnp.float32
BF16 = jnp.bfloat16


def row_sums(panel, refl):
    return lax.dot_general(panel, refl, (((0,), (0,)), ((), ())), preferred_element_type=F32)


def times_coeffs(refl, coeffs_t):
    return lax.dot_general(refl, coeffs_t, (((1,), (1,)), ((), ())), preferred_element_type=F32)


VMEM = pl.BlockSpec(memory_space=pltpu.VMEM)
SMEM = pl.BlockSpec(memory_space=pltpu.SMEM)
HBM = pl.BlockSpec(memory_space=pltpu.MemorySpace.HBM)
DMA = pltpu.SemaphoreType.DMA


def local_call(kernel, outs, held=(), numbers=(), far=(), scratch=()):
    held = [pltpu.with_memory_space_constraint(a, pltpu.VMEM) for a in held]
    far = [pltpu.with_memory_space_constraint(a, pltpu.MemorySpace.HBM) for a in far]
    return pl.pallas_call(
        kernel,
        in_specs=[SMEM] * len(numbers) + [VMEM] * len(held) + [HBM] * len(far),
        out_specs=[spec for spec, _ in outs],
        out_shape=[shape for _, shape in outs],
        scratch_shapes=list(scratch),
        compiler_params=pltpu.CompilerParams(vmem_limit_bytes=12 << 20),
    )(*numbers, *held, *far)


def in_vmem(shape, dtype=BF16):
    return VMEM, pltpu.VMEM(shape, dtype)


def in_smem(count):
    return SMEM, jax.ShapeDtypeStruct((count,), jnp.int32)


def rows_at(block, count=1):
    return pl.ds(pl.multiple_of(block * BLOCK, BLOCK), count * BLOCK)


def root_partial(panel, refl, route_root, route_mid):
    rows = panel.shape[0]
    steps = rows // TILE
    slots = FRONTS * CAP

    def place_blocks(route_ref, table_ref, seen_ref):
        for goal in range(FRONTS):
            seen_ref[goal] = 0

        def body(i, _):
            goal = route_ref[i]
            table_ref[goal * CAP + seen_ref[goal]] = i
            seen_ref[goal] = seen_ref[goal] + 1
            return 0

        lax.fori_loop(0, route_ref.shape[0], body, 0)

    def kernel(
        g_far, y_far, r0_far, r1_far, out_ref, g_ref, y_ref, t0_ref, t1_ref, tall_ref, acc_ref, seen_ref, r0_ref, r1_ref, sems, route_sems
    ):
        routes = [
            pltpu.make_async_copy(r0_far, r0_ref, route_sems.at[0]),
            pltpu.make_async_copy(r1_far, r1_ref, route_sems.at[1]),
        ]
        for copy in routes:
            copy.start()

        def copies(i):
            at = pl.ds(i * TILE, TILE)
            return [
                pltpu.make_async_copy(far.at[at], near.at[at], sems.at[k, i])
                for k, (far, near) in enumerate(((y_far, y_ref), (g_far, g_ref)))
            ]

        for i in range(steps):
            for copy in copies(i):
                copy.start()
        for i in range(slots):
            t0_ref[i] = -1
        for copy in routes:
            copy.wait()
        place_blocks(r0_ref, t0_ref, seen_ref)
        place_blocks(r1_ref, t1_ref, seen_ref)
        for i in range(steps):
            for copy in copies(i):
                copy.wait()
            at = slice(i * TILE, (i + 1) * TILE)
            part = row_sums(g_ref[at, :], y_ref[at, :])
            acc_ref[...] = part if i == 0 else acc_ref[...] + part
        for j in range(4):
            tall_ref[pl.ds(j, COLS, stride=4), :] = acc_ref[:, 128 * j : 128 * (j + 1)]
        out_ref[...] = tall_ref[...].astype(BF16)

    return local_call(
        kernel,
        [in_vmem((COLS * 4, 128)), in_vmem((rows, COLS)), in_vmem((rows, REFL))]
        + [in_smem(slots), in_smem(slots)],
        far=[panel, refl, route_root, route_mid],
        scratch=[
            pltpu.VMEM((COLS * 4, 128), F32),
            pltpu.VMEM((COLS, REFL), F32),
            pltpu.SMEM((FRONTS,), jnp.int32),
            pltpu.SMEM(route_root.shape, jnp.int32),
            pltpu.SMEM(route_mid.shape, jnp.int32),
            DMA((2, steps)),
            DMA((2,)),
        ],
    )


def ring_index(shift):
    return jnp.bitwise_and(lax.axis_index("front") + shift, FRONTS - 1)


def staged(refl, triangle, after, table):
    ordered = table is not None
    slots = FRONTS * CAP

    def kernel(*refs):
        if ordered:
            _, table_ref, y_far, t_far, y_ref, high_ref, low_ref, order_ref, t_ref, sems, order_sems = refs
        else:
            _, y_far, t_far, y_ref, high_ref, low_ref, t_ref, sems = refs
        triangle_copy = pltpu.make_async_copy(t_far, t_ref, sems.at[0])
        refl_copy = pltpu.make_async_copy(y_far, y_ref, sems.at[1])
        triangle_copy.start()
        refl_copy.start()
        triangle_copy.wait()
        high, low = split_bf16(t_ref[...])
        high_ref[...] = high
        low_ref[...] = low
        if ordered:
            blocks = [
                pltpu.make_async_copy(
                    y_far.at[rows_at(table_ref[k])],
                    order_ref.at[pl.ds(k * BLOCK, BLOCK)],
                    order_sems.at[k],
                )
                for k in range(slots)
            ]
            for copy in blocks:
                copy.start()
            for copy in blocks:
                copy.wait()
        refl_copy.wait()

    return local_call(
        kernel,
        [in_vmem(refl.shape)] + [in_vmem((REFL, REFL))] * 2 + ([in_vmem(refl.shape)] if ordered else []),
        numbers=[after] + ([table] if ordered else []),
        far=[refl, triangle],
        scratch=[pltpu.VMEM((REFL, REFL), F32), DMA((2,))] + ([DMA((slots,))] if ordered else []),
    )


def front_partial(chunks, refl, before, last):
    shifts = list(chunks)
    ahead = [] if before is None else [before]

    def kernel(*refs):
        y_ref, out_ref, acc_ref = refs[-3], refs[-2], refs[-1]
        total = acc_ref if last else out_ref
        for k, d in enumerate(shifts):
            rows = y_ref[rows_at(ring_index(-d) * CAP, CAP), :]
            part = row_sums(refs[k][:CHUNK, :], rows)
            if k == 0 and before is not None:
                part = part + refs[len(shifts)][...]
            total[...] = part if k == 0 else total[...] + part
        if last:
            out_ref[...] = acc_ref[...].astype(BF16)

    return local_call(
        kernel,
        [in_vmem((COLS, REFL), BF16 if last else F32)],
        [*chunks.values(), *ahead, refl],
        scratch=[pltpu.VMEM((COLS, REFL), F32)],
    )[0]


def split_bf16(x):
    high = x.astype(BF16)
    return high, (x - high.astype(F32)).astype(BF16)


def fine_dot(a, b_high, b_low):
    a_high, a_low = split_bf16(a)
    dot = lambda u, v: jnp.dot(u, v, preferred_element_type=F32)
    return dot(a_high, b_high) + (dot(a_low, b_high) + dot(a_high, b_low))


def root_share(arrived, triangle):
    def kernel(x_ref, t_ref, out_ref):
        total = jnp.sum(x_ref[...].astype(F32), axis=0)
        rows = [jnp.concatenate([total[4 * c + j : 4 * c + j + 1] for j in range(4)], 1) for c in range(2)]
        both = jnp.concatenate(rows + [jnp.zeros((6, REFL), F32)], axis=0)
        coeffs = fine_dot(both, *split_bf16(t_ref[...]))
        chunk = jnp.concatenate(
            [coeffs[c : c + 1, 128 * j : 128 * (j + 1)] for c in range(2) for j in range(4)], 0
        )
        out_ref[...] = jnp.broadcast_to(chunk.astype(BF16)[None], out_ref.shape)

    return local_call(kernel, [in_vmem(arrived.shape)], [arrived, triangle])[0]


def front_share(arrived, high, low):
    def kernel(x_ref, high_ref, low_ref, out_ref):
        total = jnp.sum(x_ref[...].astype(F32), axis=0)
        coeffs = fine_dot(total, high_ref[...], low_ref[...]).astype(BF16)
        out_ref[...] = jnp.broadcast_to(coeffs[None], out_ref.shape)

    return local_call(kernel, [in_vmem(arrived.shape)], [arrived, high, low])[0]


LEAVING = in_vmem((CHUNK + FLAGS, COLS))


def leave(pick_panel, flags, pick_refl, ct_ref, out_ref):
    for i in range(CHUNK // TILE):
        update = times_coeffs(pick_refl(i), ct_ref[...])
        for b in range(TILE // BLOCK):
            p = i * (TILE // BLOCK) + b
            new = (pick_panel(p).astype(F32) - update[b * BLOCK : (b + 1) * BLOCK, :]) * flags[p]
            out_ref[p * BLOCK : (p + 1) * BLOCK, :] = new.astype(BF16)
    rows = flags + [jnp.zeros((FLAGS - CAP, COLS), F32)]
    out_ref[CHUNK:, :] = jnp.concatenate(rows, axis=0).astype(BF16)


def root_leave(shift, coeffs, panel, refl, table, first):
    def kernel(t_ref, c_ref, g_ref, y_ref, out_ref, *rest):
        if first:
            ct_ref, token_ref, tall_ref, ys_ref = rest
            token_ref[0] = 0
            tall_ref[...] = c_ref[...].astype(F32)
            for j in range(4):
                ct_ref[:, 128 * j : 128 * (j + 1)] = tall_ref[pl.ds(j, COLS, stride=4), :].astype(BF16)
        else:
            ct_ref, (ys_ref,) = c_ref, rest
        goal = ring_index(shift) * CAP
        at = [t_ref[goal + p] for p in range(CAP)]
        rows = [rows_at(jnp.maximum(k, 0)) for k in at]
        for p in range(CAP):
            ys_ref[p * BLOCK : (p + 1) * BLOCK, :] = y_ref[rows[p], :]
        flags = [jnp.broadcast_to(jnp.where(k >= 0, 1.0, 0.0).astype(F32), (1, COLS)) for k in at]
        leave(
            lambda p: g_ref[rows[p], :],
            flags,
            lambda i: ys_ref[i * TILE : (i + 1) * TILE, :],
            ct_ref,
            out_ref,
        )

    return local_call(
        kernel,
        [LEAVING] + ([in_vmem((COLS, REFL)), in_smem(1)] if first else []),
        [coeffs, panel, refl],
        [table],
        scratch=([pltpu.VMEM((COLS * 4, 128), F32)] if first else []) + [pltpu.VMEM((CHUNK, REFL), BF16)],
    )


def front_leave(shift, coeffs, chunks, ordered, table, first):
    def kernel(t_ref, c_ref, g0, g1, g2, g3, y_ref, out_ref, *rest):
        *token, gs_ref, flag_ref = rest
        for token_ref in token:
            token_ref[0] = 0
        for d, g_ref in enumerate((g0, g1, g2, g3)):
            flag_ref[d * FLAGS : (d + 1) * FLAGS, :] = g_ref[CHUNK:, :].astype(F32)
        goal = ring_index(shift) * CAP
        flags = []
        for p in range(CAP):
            block = t_ref[goal + p]
            chunk, place = ring_index(-(block // CAP)), block % CAP
            for d, g_ref in enumerate((g0, g1, g2, g3)):

                @pl.when(chunk == d)
                def _():
                    gs_ref[p * BLOCK : (p + 1) * BLOCK, :] = g_ref[rows_at(place), :]

            flags.append(flag_ref[pl.ds(chunk * FLAGS + place, 1), :])
        leave(
            lambda p: gs_ref[p * BLOCK : (p + 1) * BLOCK, :],
            flags,
            lambda i: y_ref[rows_at(goal + i * (TILE // BLOCK), TILE // BLOCK), :],
            c_ref,
            out_ref,
        )

    return local_call(
        kernel,
        [LEAVING] + ([in_smem(1)] if first else []),
        [coeffs, *chunks, ordered],
        [table],
        scratch=[pltpu.VMEM((CHUNK, COLS), BF16), pltpu.VMEM((FRONTS * FLAGS, COLS), F32)],
    )


def leaf_apply(coeffs, chunks, refl):
    per = CHUNK // TILE
    blocks = TILE // BLOCK

    def kernel(c_ref, g0, g1, g2, g3, y_ref, out_far, new_ref, sems):
        def leaving(d, i):
            return pltpu.make_async_copy(
                new_ref.at[pl.ds((d * per + i) * TILE, TILE)],
                out_far.at[rows_at(ring_index(-d) * CAP + i * blocks, blocks)],
                sems.at[d * per + i],
            )

        for d, g_ref in enumerate((g0, g1, g2, g3)):
            flags = g_ref[CHUNK:, :].astype(F32)
            for i in range(per):
                rows = rows_at(ring_index(-d) * CAP + i * blocks, blocks)
                update = times_coeffs(y_ref[rows, :], c_ref[...])
                for b in range(blocks):
                    p = i * blocks + b
                    old = g_ref[p * BLOCK : (p + 1) * BLOCK, :].astype(F32)
                    new = (old - update[b * BLOCK : (b + 1) * BLOCK, :]) * flags[p : p + 1, :]
                    at = d * CHUNK + p * BLOCK
                    new_ref[at : at + BLOCK, :] = new.astype(BF16)
                leaving(d, i).start()
        for d in range(FRONTS):
            for i in range(per):
                leaving(d, i).wait()

    return local_call(
        kernel,
        [(HBM, jax.ShapeDtypeStruct((FRONTS * CHUNK, COLS), BF16))],
        [coeffs, *chunks, refl],
        scratch=[pltpu.VMEM((FRONTS * CHUNK, COLS), BF16), DMA((FRONTS * per,))],
    )[0]


def all_to_all(x, axes):
    return lax.all_to_all(x, axes, 0, 0, tiled=True)


def shifted(x, d):
    return lax.ppermute(x, "front", [(i, (i + d) % FRONTS) for i in range(FRONTS)])


ORDER = (2, 1, 3)


def route(leaving):
    chunks = {}
    for d in ORDER + (0,):
        out = leaving(d)
        chunks[d] = shifted(out, d) if d else out
    return [chunks[d] for d in range(FRONTS)]


def front_level(chunks, refl, high, low):
    partial = None
    for group in ((0,), (2,), (1, 3)):
        partial = front_partial({d: chunks[d] for d in group}, refl, partial, group == (1, 3))
    arrived = all_to_all(partial.reshape(32, COLS // 32, REFL), ROWS)
    return all_to_all(front_share(arrived, high, low), ROWS).reshape(COLS, REFL)


def per_device(
    panel_g, refl_root, refl_mid, refl_leaf, tri_root, tri_mid, tri_leaf, route_root, route_mid
):
    panel = panel_g.reshape(-1, COLS)
    y_root, y_mid, y_leaf = (y.reshape(-1, REFL) for y in (refl_root, refl_mid, refl_leaf))

    partial, panel, y_root, root_table, mid_table = root_partial(
        panel, y_root, route_root.reshape(-1), route_mid.reshape(-1)
    )
    arrived = all_to_all(partial.reshape(128, 8, 128), ALL)
    coeffs = all_to_all(root_share(arrived, tri_root), ALL).reshape(COLS * 4, 128)
    token = None

    def from_root(d):
        nonlocal coeffs, token
        out = root_leave(d, coeffs, panel, y_root, root_table, token is None)
        if token is None:
            _, coeffs, token = out
        return out[0]

    chunks = route(from_root)
    y_mid, high, low, ordered = staged(y_mid, tri_mid[0], token, mid_table)
    coeffs = front_level(chunks, y_mid, high, low)
    arrived, token = chunks, None

    def from_middle(d):
        nonlocal token
        out = front_leave(d, coeffs, arrived, ordered, mid_table, token is None)
        if token is None:
            token = out[1]
        return out[0]

    chunks = route(from_middle)
    y_leaf, high, low = staged(y_leaf, tri_leaf[0], token, None)
    coeffs = front_level(chunks, y_leaf, high, low)
    out = leaf_apply(coeffs, chunks, y_leaf)
    return out.reshape(refl_leaf.shape[:3] + (COLS,))


def solution(mesh):
    finer = Mesh(
        mesh.devices.reshape(mesh.shape["front"], 4, 4, 2), ("front", "rows_0", "rows_1", "rows_2")
    )
    rows = P("front", ROWS, None, None)
    placed = (
        rows,
        rows,
        rows,
        rows,
        P(),
        P("front", None, None),
        P("front", None, None),
        P("front", ROWS, None),
        P("front", ROWS, None),
    )
    return jax.shard_map(
        per_device,
        mesh=finer,
        in_specs=placed,
        out_specs=rows,
        check_vma=False,
    )
```

profile of v0, /device:TPU:1, one launch (start us, length us, event | category | flops | bytes accessed | tf_op | source)
XLA Modules:
  0.0 153.5 jit_solution(15181433666446710322)
XLA Ops:
  0.0 0.0 copy-start
  0.0 2.8 %shard_map.91 = (bf16[1024,128]{1,0:T(8,128)(2,1)S(1)}, bf16[2048,256]{1,0:T(8,128)(2,1)S(1)}, bf16[2048,512]{1,0:T(8,128)(2,1)S(1)}, s32[32]{0:T(128)S(1)}, s32[32]{0:T(128)S(1)}) custom-call(bf16[2048,256]{1,0:T(8,128)(2,1)} %bitcast.27, bf16[2048,512]{1,0:T(8,128)(2,1)} %bitcast.26, s32[16]{0:T(128)} %bitcast.30, s32[32]{0:T(128)} %bitcast.31), custom_call_target="tpu_custom_call" | custom-call | tf_op jit(solution)/shard_map/pallas_call | solution.py:41
  2.8 22.2 %all_to_all.30.x_ref = bf16[128,8,128]{2,1,0:T(8,128)(2,1)S(1)} all-to-all(bf16[128,8,128]{2,1,0:T(8,128)(2,1)S(1)} %bitcast.23), channel_id=1, replica_groups=mesh['front'=4,'rows_0'=4,'rows_1'=4,'rows_2'=2] {'front','rows_0','rows..., dimensions={0} | all-to-all | bytes 524288 | tf_op jit(solution)/shard_map/all_to_all | solution.py:356
  24.9 0.0 copy-done
  24.9 0.5 shard_map.92
  25.4 15.3 %all_to_all.31 = bf16[128,8,128]{2,1,0:T(8,128)(2,1)S(1)} all-to-all(bf16[128,8,128]{2,1,0:T(8,128)(2,1)S(1)} %shard_map.92), channel_id=1, replica_groups=mesh['front'=4,'rows_0'=4,'rows_1'=4,'rows_2'=2] {'front','rows_0','rows..., dimensions={0} | all-to-all | bytes 524288 | tf_op jit(solution)/shard_map/all_to_all | solution.py:356
  40.7 1.3 shard_map.93
  42.1 1.0 shard_map.95
  43.1 1.3 collective-permute-start.2
  44.4 1.0 shard_map.94
  45.4 0.1 collective-permute-start
  45.6 2.6 %collective-permute-start.1 = (bf16[1040,256]{1,0:T(8,128)(2,1)S(1)}, bf16[1040,256]{1,0:T(8,128)(2,1)S(1)}, u32[]{:S(2)}, u32[]{:S(2)}) collective-permute-start(bf16[1040,256]{1,0:T(8,128)(2,1)S(1)} %shard_map.95), channel_id=1, source_target_pairs={{0,96},{32,0},{64,32},{96,64},{1,97},{33,1},{65,33},{97,65},{2,98}... | collective-permute-start | bytes 1597448 | tf_op jit(solution)/shard_map/ppermute | solution.py:360
  48.2 1.0 shard_map.96.refs_0_.g0
  49.2 5.3 %shard_map.97 = (bf16[4096,512]{1,0:T(8,128)(2,1)S(1)}, bf16[512,512]{1,0:T(8,128)(2,1)S(1)}, bf16[512,512]{1,0:T(8,128)(2,1)S(1)}, bf16[4096,512]{1,0:T(8,128)(2,1)S(1)}) custom-call(s32[1]{0:T(128)} %get-tuple-element.29.refs_0_, s32[32]{0:T(128)S(1)} %get-tuple-element.22.refs_1_.t_ref, bf16[4096,512]{1,0:T(8,128)(2,1)} %bitcast.24, f32[512,512]{1,0:T(8,128)} %bitcast.28), custom_call_target="tpu_custom_call" | custom-call | tf_op jit(solution)/shard_map/pallas_call | solution.py:41
  54.5 0.5 shard_map.98.refs_1_
  55.0 2.5 %collective-permute-done.2.refs_0_.g2 = bf16[1040,256]{1,0:T(8,128)(2,1)S(1)} collective-permute-done((bf16[1040,256]{1,0:T(8,128)(2,1)S(1)}, bf16[1040,256]{1,0:T(8,128)(2,1)S(1)}, u32[]{:S(2)}, u32[]{:S(2)}) %collective-permute-start.2) | collective-permute-done | bytes 532512 | tf_op jit(solution)/shard_map/ppermute | solution.py:360
  57.5 0.5 shard_map.99.refs_2_
  58.0 12.1 %collective-permute-done.refs_0_.g1 = bf16[1040,256]{1,0:T(8,128)(2,1)S(1)} collective-permute-done((bf16[1040,256]{1,0:T(8,128)(2,1)S(1)}, bf16[1040,256]{1,0:T(8,128)(2,1)S(1)}, u32[]{:S(2)}, u32[]{:S(2)}) %collective-permute-start) | collective-permute-done | bytes 532512 | tf_op jit(solution)/shard_map/ppermute | solution.py:360
  70.1 0.0 collective-permute-done.1.refs_1_.g3
  70.1 0.7 shard_map.100
  70.9 13.0 %all_to_all.32.x_ref = bf16[32,8,512]{2,1,0:T(8,128)(2,1)S(1)} all-to-all(bf16[32,8,512]{2,1,0:T(8,128)(2,1)S(1)} %bitcast.21), channel_id=1, replica_groups=mesh['front'=4,'rows_0'=4,'rows_1'=4,'rows_2'=2] {'rows_0','rows_1','row..., dimensions={0} | all-to-all | bytes 524288 | tf_op jit(solution)/shard_map/all_to_all | solution.py:356
  83.8 0.4 shard_map.101
  84.2 12.4 %all_to_all.33 = bf16[32,8,512]{2,1,0:T(8,128)(2,1)S(1)} all-to-all(bf16[32,8,512]{2,1,0:T(8,128)(2,1)S(1)} %shard_map.101), channel_id=1, replica_groups=mesh['front'=4,'rows_0'=4,'rows_1'=4,'rows_2'=2] {'rows_0','rows_1','row..., dimensions={0} | all-to-all | bytes 524288 | tf_op jit(solution)/shard_map/all_to_all | solution.py:356
  96.6 1.4 shard_map.104
  98.0 0.7 collective-permute-start.5
  98.7 1.3 shard_map.102
  100.0 0.5 collective-permute-start.3
  100.5 1.3 shard_map.103
  101.8 2.3 %collective-permute-start.4 = (bf16[1040,256]{1,0:T(8,128)(2,1)S(1)}, bf16[1040,256]{1,0:T(8,128)(2,1)S(1)}, u32[]{:S(2)}, u32[]{:S(2)}) collective-permute-start(bf16[1040,256]{1,0:T(8,128)(2,1)S(1)} %shard_map.103), channel_id=1, source_target_pairs={{0,96},{32,0},{64,32},{96,64},{1,97},{33,1},{65,33},{97,65},{2,98}... | collective-permute-start | bytes 1597448 | tf_op jit(solution)/shard_map/ppermute | solution.py:360
  104.1 3.2 %shard_map.106 = (bf16[4096,512]{1,0:T(8,128)(2,1)S(1)}, bf16[512,512]{1,0:T(8,128)(2,1)S(1)}, bf16[512,512]{1,0:T(8,128)(2,1)S(1)}) custom-call(s32[1]{0:T(128)} %get-tuple-element.35.refs_0_, bf16[4096,512]{1,0:T(8,128)(2,1)} %bitcast.25, f32[512,512]{1,0:T(8,128)} %bitcast.29), custom_call_target="tpu_custom_call" | custom-call | tf_op jit(solution)/shard_map/pallas_call | solution.py:41
  107.3 1.3 shard_map.105.refs_0_.g0
  108.6 0.5 shard_map.107.refs_1_
  109.1 4.0 %collective-permute-done.5.refs_0_.g2 = bf16[1040,256]{1,0:T(8,128)(2,1)S(1)} collective-permute-done((bf16[1040,256]{1,0:T(8,128)(2,1)S(1)}, bf16[1040,256]{1,0:T(8,128)(2,1)S(1)}, u32[]{:S(2)}, u32[]{:S(2)}) %collective-permute-start.5) | collective-permute-done | bytes 532512 | tf_op jit(solution)/shard_map/ppermute | solution.py:360
  113.1 0.5 shard_map.108.refs_2_
  113.6 11.4 %collective-permute-done.3.refs_0_.g1 = bf16[1040,256]{1,0:T(8,128)(2,1)S(1)} collective-permute-done((bf16[1040,256]{1,0:T(8,128)(2,1)S(1)}, bf16[1040,256]{1,0:T(8,128)(2,1)S(1)}, u32[]{:S(2)}, u32[]{:S(2)}) %collective-permute-start.3) | collective-permute-done | bytes 532512 | tf_op jit(solution)/shard_map/ppermute | solution.py:360
  125.0 0.0 collective-permute-done.4.refs_1_.g3
  125.0 0.7 shard_map.109
  125.8 12.6 %all_to_all.34.x_ref = bf16[32,8,512]{2,1,0:T(8,128)(2,1)S(1)} all-to-all(bf16[32,8,512]{2,1,0:T(8,128)(2,1)S(1)} %bitcast.22), channel_id=1, replica_groups=mesh['front'=4,'rows_0'=4,'rows_1'=4,'rows_2'=2] {'rows_0','rows_1','row..., dimensions={0} | all-to-all | bytes 524288 | tf_op jit(solution)/shard_map/all_to_all | solution.py:356
  138.4 0.4 shard_map.110
  138.7 12.4 %all_to_all.35 = bf16[32,8,512]{2,1,0:T(8,128)(2,1)S(1)} all-to-all(bf16[32,8,512]{2,1,0:T(8,128)(2,1)S(1)} %shard_map.110), channel_id=1, replica_groups=mesh['front'=4,'rows_0'=4,'rows_1'=4,'rows_2'=2] {'rows_0','rows_1','row..., dimensions={0} | all-to-all | bytes 524288 | tf_op jit(solution)/shard_map/all_to_all | solution.py:356
  151.2 2.3 %shard_map.111 = bf16[4096,256]{1,0:T(8,128)(2,1)} custom-call(bf16[256,512]{1,0:T(8,128)(2,1)S(1)} %bitcast.19, bf16[1040,256]{1,0:T(8,128)(2,1)S(1)} %shard_map.105.refs_0_.g0, bf16[1040,256]{1,0:T(8,128)(2,1)S(1)} %collective-permute-done.3.refs_0_.g1, bf16[1040,256]{1,0:T(8,128)(2,1)S(1)} %collective-permute-done.5.refs_0_.g2, ...), custom_call_target="tpu_custom_call" | custom-call | tf_op jit(solution)/shard_map/pallas_call | solution.py:41
Async XLA Ops:
  0.0 24.9 %copy-start = (f32[512,512]{1,0:T(8,128)S(1)}, f32[512,512]{1,0:T(8,128)}, u32[]{:S(2)}) copy-start(f32[512,512]{1,0:T(8,128)} %t_ref.1) | copy-start | bytes 3145732
  43.1 14.4 %collective-permute-start.2 = (bf16[1040,256]{1,0:T(8,128)(2,1)S(1)}, bf16[1040,256]{1,0:T(8,128)(2,1)S(1)}, u32[]{:S(2)}, u32[]{:S(2)}) collective-permute-start(bf16[1040,256]{1,0:T(8,128)(2,1)S(1)} %get-tuple-element.28), channel_id=1, source_target_pairs={{0,64},{32,96},{64,0},{96,32},{1,65},{33,97},{65,1},{97,33},{2,66}... | collective-permute-start | bytes 1597448 | tf_op jit(solution)/shard_map/ppermute | solution.py:360
  45.4 24.7 %collective-permute-start = (bf16[1040,256]{1,0:T(8,128)(2,1)S(1)}, bf16[1040,256]{1,0:T(8,128)(2,1)S(1)}, u32[]{:S(2)}, u32[]{:S(2)}) collective-permute-start(bf16[1040,256]{1,0:T(8,128)(2,1)S(1)} %shard_map.94), channel_id=1, source_target_pairs={{0,32},{32,64},{64,96},{96,0},{1,33},{33,65},{65,97},{97,1},{2,34}... | collective-permute-start | bytes 1597448 | tf_op jit(solution)/shard_map/ppermute | solution.py:360
  45.6 24.5 %collective-permute-start.1 = (bf16[1040,256]{1,0:T(8,128)(2,1)S(1)}, bf16[1040,256]{1,0:T(8,128)(2,1)S(1)}, u32[]{:S(2)}, u32[]{:S(2)}) collective-permute-start(bf16[1040,256]{1,0:T(8,128)(2,1)S(1)} %shard_map.95), channel_id=1, source_target_pairs={{0,96},{32,0},{64,32},{96,64},{1,97},{33,1},{65,33},{97,65},{2,98}... | collective-permute-start | bytes 1597448 | tf_op jit(solution)/shard_map/ppermute | solution.py:360
  98.0 15.1 %collective-permute-start.5 = (bf16[1040,256]{1,0:T(8,128)(2,1)S(1)}, bf16[1040,256]{1,0:T(8,128)(2,1)S(1)}, u32[]{:S(2)}, u32[]{:S(2)}) collective-permute-start(bf16[1040,256]{1,0:T(8,128)(2,1)S(1)} %get-tuple-element.34), channel_id=1, source_target_pairs={{0,64},{32,96},{64,0},{96,32},{1,65},{33,97},{65,1},{97,33},{2,66}... | collective-permute-start | bytes 1597448 | tf_op jit(solution)/shard_map/ppermute | solution.py:360
  100.0 25.0 %collective-permute-start.3 = (bf16[1040,256]{1,0:T(8,128)(2,1)S(1)}, bf16[1040,256]{1,0:T(8,128)(2,1)S(1)}, u32[]{:S(2)}, u32[]{:S(2)}) collective-permute-start(bf16[1040,256]{1,0:T(8,128)(2,1)S(1)} %shard_map.102), channel_id=1, source_target_pairs={{0,32},{32,64},{64,96},{96,0},{1,33},{33,65},{65,97},{97,1},{2,34}... | collective-permute-start | bytes 1597448 | tf_op jit(solution)/shard_map/ppermute | solution.py:360
  101.8 23.2 %collective-permute-start.4 = (bf16[1040,256]{1,0:T(8,128)(2,1)S(1)}, bf16[1040,256]{1,0:T(8,128)(2,1)S(1)}, u32[]{:S(2)}, u32[]{:S(2)}) collective-permute-start(bf16[1040,256]{1,0:T(8,128)(2,1)S(1)} %shard_map.103), channel_id=1, source_target_pairs={{0,96},{32,0},{64,32},{96,64},{1,97},{33,1},{65,33},{97,65},{2,98}... | collective-permute-start | bytes 1597448 | tf_op jit(solution)/shard_map/ppermute | solution.py:360
where the time goes:
time: 154 us; the launch traced here: 153 us
  blocking collectives  87.9 us (57%)
  waiting for transfers between devices  30.1 us (20%)
  Pallas kernels  27.7 us (18%)
  starting transfers between devices  7.61 us (5%)
    all_to_all x6, blocking collectives, all_to_all(): return lax.all_to_all(x, axes, 0, 0, tiled=True)  87.9 us
    ppermute x6, waiting for transfers between devices, shifted(): lax.ppermute(x, 'front', [(i, (i + d) % FRONTS) for i in range(FRONTS)])  30.1 us
    pallas_call x21, Pallas kernels, local_call(): pl.pallas_call(kernel, in_specs=[SMEM] * len(numbers) + [VMEM] * len(held...  27.7 us
    ppermute x6, starting transfers between devices, shifted(): lax.ppermute(x, 'front', [(i, (i + d) % FRONTS) for i in range(FRONTS)])  7.61 us
  transfers between devices with their start and end apart: 6, of which 4 were waited for; matrix products, arithmetic and copies ran while one was open for 0% of the time, Pallas kernels for 11%

commit v1 on v0

--- a/solution.py
+++ b/solution.py
@@ -140,17 +140,14 @@
 
     def kernel(*refs):
         if ordered:
-            _, table_ref, y_far, t_far, y_ref, high_ref, low_ref, order_ref, t_ref, sems, order_sems = refs
+            _, table_ref, y_far, t_far, order_ref, v_ref, y_ref, t_ref, sems, order_sems = refs
         else:
-            _, y_far, t_far, y_ref, high_ref, low_ref, t_ref, sems = refs
+            _, y_far, t_far, y_ref, v_ref, t_ref, sems = refs
         triangle_copy = pltpu.make_async_copy(t_far, t_ref, sems.at[0])
         refl_copy = pltpu.make_async_copy(y_far, y_ref, sems.at[1])
         triangle_copy.start()
         refl_copy.start()
-        triangle_copy.wait()
-        high, low = split_bf16(t_ref[...])
-        high_ref[...] = high
-        low_ref[...] = low
+        blocks = []
         if ordered:
             blocks = [
                 pltpu.make_async_copy(
@@ -162,16 +159,23 @@
             ]
             for copy in blocks:
                 copy.start()
-            for copy in blocks:
-                copy.wait()
+        triangle_copy.wait()
         refl_copy.wait()
-
-    return local_call(
-        kernel,
-        [in_vmem(refl.shape)] + [in_vmem((REFL, REFL))] * 2 + ([in_vmem(refl.shape)] if ordered else []),
+        high, low = split_bf16(t_ref[...])
+        for i in range(slots * BLOCK // TILE):
+            at = slice(i * TILE, (i + 1) * TILE)
+            dot = lambda t: jnp.dot(y_ref[at, :], t, preferred_element_type=F32)
+            v_ref[at, :] = (dot(high) + dot(low)).astype(BF16)
+        for copy in blocks:
+            copy.wait()
+
+    held = [pltpu.VMEM(refl.shape, BF16)] if ordered else []
+    return local_call(
+        kernel,
+        [in_vmem(refl.shape)] * 2,
         numbers=[after] + ([table] if ordered else []),
         far=[refl, triangle],
-        scratch=[pltpu.VMEM((REFL, REFL), F32), DMA((2,))] + ([DMA((slots,))] if ordered else []),
+        scratch=held + [pltpu.VMEM((REFL, REFL), F32), DMA((2,))] + ([DMA((slots,))] if ordered else []),
     )
 
 
@@ -224,13 +228,12 @@
     return local_call(kernel, [in_vmem(arrived.shape)], [arrived, triangle])[0]
 
 
-def front_share(arrived, high, low):
-    def kernel(x_ref, high_ref, low_ref, out_ref):
-        total = jnp.sum(x_ref[...].astype(F32), axis=0)
-        coeffs = fine_dot(total, high_ref[...], low_ref[...]).astype(BF16)
-        out_ref[...] = jnp.broadcast_to(coeffs[None], out_ref.shape)
-
-    return local_call(kernel, [in_vmem(arrived.shape)], [arrived, high, low])[0]
+def front_share(arrived):
+    def kernel(x_ref, out_ref):
+        total = jnp.sum(x_ref[...].astype(F32), axis=0).astype(BF16)
+        out_ref[...] = jnp.broadcast_to(total[None], out_ref.shape)
+
+    return local_call(kernel, [in_vmem(arrived.shape)], [arrived])[0]
 
 
 LEAVING = in_vmem((CHUNK + FLAGS, COLS))
@@ -371,12 +374,12 @@
     return [chunks[d] for d in range(FRONTS)]
 
 
-def front_level(chunks, refl, high, low):
+def front_level(chunks, refl):
     partial = None
     for group in ((0,), (2,), (1, 3)):
         partial = front_partial({d: chunks[d] for d in group}, refl, partial, group == (1, 3))
     arrived = all_to_all(partial.reshape(32, COLS // 32, REFL), ROWS)
-    return all_to_all(front_share(arrived, high, low), ROWS).reshape(COLS, REFL)
+    return all_to_all(front_share(arrived), ROWS).reshape(COLS, REFL)
 
 
 def per_device(
@@ -400,8 +403,8 @@
         return out[0]
 
     chunks = route(from_root)
-    y_mid, high, low, ordered = staged(y_mid, tri_mid[0], token, mid_table)
-    coeffs = front_level(chunks, y_mid, high, low)
+    ordered, v_mid = staged(y_mid, tri_mid[0], token, mid_table)
+    coeffs = front_level(chunks, v_mid)
     arrived, token = chunks, None
 
     def from_middle(d):
@@ -412,8 +415,8 @@
         return out[0]
 
     chunks = route(from_middle)
-    y_leaf, high, low = staged(y_leaf, tri_leaf[0], token, None)
-    coeffs = front_level(chunks, y_leaf, high, low)
+    y_leaf, v_leaf = staged(y_leaf, tri_leaf[0], token, None)
+    coeffs = front_level(chunks, v_leaf)
     out = leaf_apply(coeffs, chunks, y_leaf)
     return out.reshape(refl_leaf.shape[:3] + (COLS,))
 

time: 154 us -> 153 us (level)
  waiting for transfers between devices: 30.1 us -> 20.8 us
  Pallas kernels: 27.7 us -> 36.1 us
    ppermute x6, waiting for transfers between devices: 30.1 us -> 20.8 us  [shifted(): lax.ppermute(x, 'front', [(i, (i + d) % FRONTS) for i in range(FRONTS)])]
    pallas_call x21, Pallas kernels: 27.7 us -> 36.1 us  [local_call(): pl.pallas_call(kernel, in_specs=[SMEM] * len(numbers) + [VMEM] * len(held...]
  transfers between devices with their start and end apart: 6 -> 6, of which waited for: 4 -> 2; matrix products, arithmetic and copies ran while one was open for 0% -> 0% of each run, Pallas kernels for 11% -> 17%
where the time goes in v1:
time: 153 us
  blocking collectives  87.9 us (57%)
  Pallas kernels  36.1 us (24%)
  waiting for transfers between devices  20.8 us (14%)
  starting transfers between devices  7.76 us (5%)
    all_to_all x6, blocking collectives, all_to_all(): return lax.all_to_all(x, axes, 0, 0, tiled=True)  87.9 us
    pallas_call x21, Pallas kernels, local_call(): pl.pallas_call(kernel, in_specs=[SMEM] * len(numbers) + [VMEM] * len(held...  36.1 us
    ppermute x6, waiting for transfers between devices, shifted(): lax.ppermute(x, 'front', [(i, (i + d) % FRONTS) for i in range(FRONTS)])  20.8 us
    ppermute x6, starting transfers between devices, shifted(): lax.ppermute(x, 'front', [(i, (i + d) % FRONTS) for i in range(FRONTS)])  7.76 us
  transfers between devices with their start and end apart: 6, of which 2 were waited for; matrix products, arithmetic and copies ran while one was open for 0% of the time, Pallas kernels for 17%

profile of v1, /device:TPU:1, one launch (start us, length us, event | category | flops | bytes accessed | tf_op | source)
XLA Modules:
  0.0 152.9 jit_solution(7819148264129882823)
XLA Ops:
  0.0 0.0 copy-start
  0.0 2.8 %shard_map.91 = (bf16[1024,128]{1,0:T(8,128)(2,1)S(1)}, bf16[2048,256]{1,0:T(8,128)(2,1)S(1)}, bf16[2048,512]{1,0:T(8,128)(2,1)S(1)}, s32[32]{0:T(128)S(1)}, s32[32]{0:T(128)S(1)}) custom-call(bf16[2048,256]{1,0:T(8,128)(2,1)} %bitcast.27, bf16[2048,512]{1,0:T(8,128)(2,1)} %bitcast.26, s32[16]{0:T(128)} %bitcast.30, s32[32]{0:T(128)} %bitcast.31), custom_call_target="tpu_custom_call" | custom-call | tf_op jit(solution)/shard_map/pallas_call | solution.py:41
  2.8 22.2 %all_to_all.30.x_ref = bf16[128,8,128]{2,1,0:T(8,128)(2,1)S(1)} all-to-all(bf16[128,8,128]{2,1,0:T(8,128)(2,1)S(1)} %bitcast.23), channel_id=1, replica_groups=mesh['front'=4,'rows_0'=4,'rows_1'=4,'rows_2'=2] {'front','rows_0','rows..., dimensions={0} | all-to-all | bytes 524288 | tf_op jit(solution)/shard_map/all_to_all | solution.py:359
  24.9 0.0 copy-done
  24.9 0.5 shard_map.92
  25.4 15.3 %all_to_all.31 = bf16[128,8,128]{2,1,0:T(8,128)(2,1)S(1)} all-to-all(bf16[128,8,128]{2,1,0:T(8,128)(2,1)S(1)} %shard_map.92), channel_id=1, replica_groups=mesh['front'=4,'rows_0'=4,'rows_1'=4,'rows_2'=2] {'front','rows_0','rows..., dimensions={0} | all-to-all | bytes 524288 | tf_op jit(solution)/shard_map/all_to_all | solution.py:359
  40.7 1.3 shard_map.93
  42.1 1.0 shard_map.95
  43.1 1.3 collective-permute-start.2
  44.4 1.0 shard_map.94
  45.4 0.2 collective-permute-start
  45.6 2.6 %collective-permute-start.1 = (bf16[1040,256]{1,0:T(8,128)(2,1)S(1)}, bf16[1040,256]{1,0:T(8,128)(2,1)S(1)}, u32[]{:S(2)}, u32[]{:S(2)}) collective-permute-start(bf16[1040,256]{1,0:T(8,128)(2,1)S(1)} %shard_map.95), channel_id=1, source_target_pairs={{0,96},{32,0},{64,32},{96,64},{1,97},{33,1},{65,33},{97,65},{2,98}... | collective-permute-start | bytes 1597448 | tf_op jit(solution)/shard_map/ppermute | solution.py:363
  48.2 1.0 shard_map.96.refs_0_.g0
  49.2 9.9 %shard_map.97 = (bf16[4096,512]{1,0:T(8,128)(2,1)S(1)}, bf16[4096,512]{1,0:T(8,128)(2,1)S(1)}) custom-call(s32[1]{0:T(128)} %get-tuple-element.26.refs_0_, s32[32]{0:T(128)S(1)} %get-tuple-element.19.refs_1_.t_ref, bf16[4096,512]{1,0:T(8,128)(2,1)} %bitcast.24, f32[512,512]{1,0:T(8,128)} %bitcast.28), custom_call_target="tpu_custom_call" | custom-call | tf_op jit(solution)/shard_map/pallas_call | solution.py:41
  59.1 0.5 shard_map.98.refs_1_
  59.6 0.0 collective-permute-done.2.refs_0_.g2
  59.6 0.5 shard_map.99.refs_2_
  60.1 10.0 %collective-permute-done.refs_0_.g1 = bf16[1040,256]{1,0:T(8,128)(2,1)S(1)} collective-permute-done((bf16[1040,256]{1,0:T(8,128)(2,1)S(1)}, bf16[1040,256]{1,0:T(8,128)(2,1)S(1)}, u32[]{:S(2)}, u32[]{:S(2)}) %collective-permute-start) | collective-permute-done | bytes 532512 | tf_op jit(solution)/shard_map/ppermute | solution.py:363
  70.1 0.0 collective-permute-done.1.refs_1_.g3
  70.1 0.7 shard_map.100
  70.9 13.0 %all_to_all.32.x_ref = bf16[32,8,512]{2,1,0:T(8,128)(2,1)S(1)} all-to-all(bf16[32,8,512]{2,1,0:T(8,128)(2,1)S(1)} %bitcast.21), channel_id=1, replica_groups=mesh['front'=4,'rows_0'=4,'rows_1'=4,'rows_2'=2] {'rows_0','rows_1','row..., dimensions={0} | all-to-all | bytes 524288 | tf_op jit(solution)/shard_map/all_to_all | solution.py:359
  83.8 0.1 shard_map.101
  83.9 12.4 %all_to_all.33 = bf16[32,8,512]{2,1,0:T(8,128)(2,1)S(1)} all-to-all(bf16[32,8,512]{2,1,0:T(8,128)(2,1)S(1)} %shard_map.101), channel_id=1, replica_groups=mesh['front'=4,'rows_0'=4,'rows_1'=4,'rows_2'=2] {'rows_0','rows_1','row..., dimensions={0} | all-to-all | bytes 524288 | tf_op jit(solution)/shard_map/all_to_all | solution.py:359
  96.3 1.4 shard_map.104
  97.7 0.7 collective-permute-start.5
  98.4 1.3 shard_map.102
  99.7 0.7 collective-permute-start.3
  100.4 1.3 shard_map.103
  101.7 2.3 %collective-permute-start.4 = (bf16[1040,256]{1,0:T(8,128)(2,1)S(1)}, bf16[1040,256]{1,0:T(8,128)(2,1)S(1)}, u32[]{:S(2)}, u32[]{:S(2)}) collective-permute-start(bf16[1040,256]{1,0:T(8,128)(2,1)S(1)} %shard_map.103), channel_id=1, source_target_pairs={{0,96},{32,0},{64,32},{96,64},{1,97},{33,1},{65,33},{97,65},{2,98}... | collective-permute-start | bytes 1597448 | tf_op jit(solution)/shard_map/ppermute | solution.py:363
  104.0 7.7 %shard_map.106 = (bf16[4096,512]{1,0:T(8,128)(2,1)S(1)}, bf16[4096,512]{1,0:T(8,128)(2,1)S(1)}) custom-call(s32[1]{0:T(128)} %get-tuple-element.30.refs_0_, bf16[4096,512]{1,0:T(8,128)(2,1)} %bitcast.25, f32[512,512]{1,0:T(8,128)} %bitcast.29), custom_call_target="tpu_custom_call" | custom-call | tf_op jit(solution)/shard_map/pallas_call | solution.py:41
  111.7 1.3 shard_map.105.refs_0_.g0
  113.0 0.5 shard_map.107.refs_1_
  113.5 0.0 collective-permute-done.5.refs_0_.g2
  113.5 0.5 shard_map.108.refs_2_
  114.0 10.8 %collective-permute-done.3.refs_0_.g1 = bf16[1040,256]{1,0:T(8,128)(2,1)S(1)} collective-permute-done((bf16[1040,256]{1,0:T(8,128)(2,1)S(1)}, bf16[1040,256]{1,0:T(8,128)(2,1)S(1)}, u32[]{:S(2)}, u32[]{:S(2)}) %collective-permute-start.3) | collective-permute-done | bytes 532512 | tf_op jit(solution)/shard_map/ppermute | solution.py:363
  124.7 0.0 collective-permute-done.4.refs_1_.g3
  124.7 0.7 shard_map.109
  125.5 12.6 %all_to_all.34.x_ref = bf16[32,8,512]{2,1,0:T(8,128)(2,1)S(1)} all-to-all(bf16[32,8,512]{2,1,0:T(8,128)(2,1)S(1)} %bitcast.22), channel_id=1, replica_groups=mesh['front'=4,'rows_0'=4,'rows_1'=4,'rows_2'=2] {'rows_0','rows_1','row..., dimensions={0} | all-to-all | bytes 524288 | tf_op jit(solution)/shard_map/all_to_all | solution.py:359
  138.1 0.1 shard_map.110
  138.1 12.4 %all_to_all.35 = bf16[32,8,512]{2,1,0:T(8,128)(2,1)S(1)} all-to-all(bf16[32,8,512]{2,1,0:T(8,128)(2,1)S(1)} %shard_map.110), channel_id=1, replica_groups=mesh['front'=4,'rows_0'=4,'rows_1'=4,'rows_2'=2] {'rows_0','rows_1','row..., dimensions={0} | all-to-all | bytes 524288 | tf_op jit(solution)/shard_map/all_to_all | solution.py:359
  150.6 2.2 %shard_map.111 = bf16[4096,256]{1,0:T(8,128)(2,1)} custom-call(bf16[256,512]{1,0:T(8,128)(2,1)S(1)} %bitcast.19, bf16[1040,256]{1,0:T(8,128)(2,1)S(1)} %shard_map.105.refs_0_.g0, bf16[1040,256]{1,0:T(8,128)(2,1)S(1)} %collective-permute-done.3.refs_0_.g1, bf16[1040,256]{1,0:T(8,128)(2,1)S(1)} %collective-permute-done.5.refs_0_.g2, ...), custom_call_target="tpu_custom_call" | custom-call | tf_op jit(solution)/shard_map/pallas_call | solution.py:41
Async XLA Ops:
  0.0 24.9 %copy-start = (f32[512,512]{1,0:T(8,128)S(1)}, f32[512,512]{1,0:T(8,128)}, u32[]{:S(2)}) copy-start(f32[512,512]{1,0:T(8,128)} %t_ref.1) | copy-start | bytes 3145732
  43.1 16.5 %collective-permute-start.2 = (bf16[1040,256]{1,0:T(8,128)(2,1)S(1)}, bf16[1040,256]{1,0:T(8,128)(2,1)S(1)}, u32[]{:S(2)}, u32[]{:S(2)}) collective-permute-start(bf16[1040,256]{1,0:T(8,128)(2,1)S(1)} %get-tuple-element.25), channel_id=1, source_target_pairs={{0,64},{32,96},{64,0},{96,32},{1,65},{33,97},{65,1},{97,33},{2,66}... | collective-permute-start | bytes 1597448 | tf_op jit(solution)/shard_map/ppermute | solution.py:363
  45.4 24.7 %collective-permute-start = (bf16[1040,256]{1,0:T(8,128)(2,1)S(1)}, bf16[1040,256]{1,0:T(8,128)(2,1)S(1)}, u32[]{:S(2)}, u32[]{:S(2)}) collective-permute-start(bf16[1040,256]{1,0:T(8,128)(2,1)S(1)} %shard_map.94), channel_id=1, source_target_pairs={{0,32},{32,64},{64,96},{96,0},{1,33},{33,65},{65,97},{97,1},{2,34}... | collective-permute-start | bytes 1597448 | tf_op jit(solution)/shard_map/ppermute | solution.py:363
  45.6 24.5 %collective-permute-start.1 = (bf16[1040,256]{1,0:T(8,128)(2,1)S(1)}, bf16[1040,256]{1,0:T(8,128)(2,1)S(1)}, u32[]{:S(2)}, u32[]{:S(2)}) collective-permute-start(bf16[1040,256]{1,0:T(8,128)(2,1)S(1)} %shard_map.95), channel_id=1, source_target_pairs={{0,96},{32,0},{64,32},{96,64},{1,97},{33,1},{65,33},{97,65},{2,98}... | collective-permute-start | bytes 1597448 | tf_op jit(solution)/shard_map/ppermute | solution.py:363
  97.7 15.8 %collective-permute-start.5 = (bf16[1040,256]{1,0:T(8,128)(2,1)S(1)}, bf16[1040,256]{1,0:T(8,128)(2,1)S(1)}, u32[]{:S(2)}, u32[]{:S(2)}) collective-permute-start(bf16[1040,256]{1,0:T(8,128)(2,1)S(1)} %get-tuple-element.29), channel_id=1, source_target_pairs={{0,64},{32,96},{64,0},{96,32},{1,65},{33,97},{65,1},{97,33},{2,66}... | collective-permute-start | bytes 1597448 | tf_op jit(solution)/shard_map/ppermute | solution.py:363
  99.7 25.0 %collective-permute-start.3 = (bf16[1040,256]{1,0:T(8,128)(2,1)S(1)}, bf16[1040,256]{1,0:T(8,128)(2,1)S(1)}, u32[]{:S(2)}, u32[]{:S(2)}) collective-permute-start(bf16[1040,256]{1,0:T(8,128)(2,1)S(1)} %shard_map.102), channel_id=1, source_target_pairs={{0,32},{32,64},{64,96},{96,0},{1,33},{33,65},{65,97},{97,1},{2,34}... | collective-permute-start | bytes 1597448 | tf_op jit(solution)/shard_map/ppermute | solution.py:363
  101.7 23.0 %collective-permute-start.4 = (bf16[1040,256]{1,0:T(8,128)(2,1)S(1)}, bf16[1040,256]{1,0:T(8,128)(2,1)S(1)}, u32[]{:S(2)}, u32[]{:S(2)}) collective-permute-start(bf16[1040,256]{1,0:T(8,128)(2,1)S(1)} %shard_map.103), channel_id=1, source_target_pairs={{0,96},{32,0},{64,32},{96,64},{1,97},{33,1},{65,33},{97,65},{2,98}... | collective-permute-start | bytes 1597448 | tf_op jit(solution)/shard_map/ppermute | solution.py:363

commit v2 on v1

--- a/solution.py
+++ b/solution.py
@@ -324,11 +324,11 @@
     blocks = TILE // BLOCK
 
     def kernel(c_ref, g0, g1, g2, g3, y_ref, out_far, new_ref, sems):
-        def leaving(d, i):
+        def leaving(d):
             return pltpu.make_async_copy(
-                new_ref.at[pl.ds((d * per + i) * TILE, TILE)],
-                out_far.at[rows_at(ring_index(-d) * CAP + i * blocks, blocks)],
-                sems.at[d * per + i],
+                new_ref.at[pl.ds(d * CHUNK, CHUNK)],
+                out_far.at[rows_at(ring_index(-d) * CAP, CAP)],
+                sems.at[d],
             )
 
         for d, g_ref in enumerate((g0, g1, g2, g3)):
@@ -342,16 +342,15 @@
                     new = (old - update[b * BLOCK : (b + 1) * BLOCK, :]) * flags[p : p + 1, :]
                     at = d * CHUNK + p * BLOCK
                     new_ref[at : at + BLOCK, :] = new.astype(BF16)
-                leaving(d, i).start()
+            leaving(d).start()
         for d in range(FRONTS):
-            for i in range(per):
-                leaving(d, i).wait()
+            leaving(d).wait()
 
     return local_call(
         kernel,
         [(HBM, jax.ShapeDtypeStruct((FRONTS * CHUNK, COLS), BF16))],
         [coeffs, *chunks, refl],
-        scratch=[pltpu.VMEM((FRONTS * CHUNK, COLS), BF16), DMA((FRONTS * per,))],
+        scratch=[pltpu.VMEM((FRONTS * CHUNK, COLS), BF16), DMA((FRONTS,))],
     )[0]
 
 

time: 153 us -> 153 us (level)
  no operation moved by 1% of the time
where the time goes in v2:
time: 153 us
  blocking collectives  87.9 us (57%)
  Pallas kernels  36 us (24%)
  waiting for transfers between devices  20.8 us (14%)
  starting transfers between devices  7.76 us (5%)
    all_to_all x6, blocking collectives, all_to_all(): return lax.all_to_all(x, axes, 0, 0, tiled=True)  87.9 us
    pallas_call x21, Pallas kernels, local_call(): pl.pallas_call(kernel, in_specs=[SMEM] * len(numbers) + [VMEM] * len(held...  36 us
    ppermute x6, waiting for transfers between devices, shifted(): lax.ppermute(x, 'front', [(i, (i + d) % FRONTS) for i in range(FRONTS)])  20.8 us
    ppermute x6, starting transfers between devices, shifted(): lax.ppermute(x, 'front', [(i, (i + d) % FRONTS) for i in range(FRONTS)])  7.76 us
  transfers between devices with their start and end apart: 6, of which 2 were waited for; matrix products, arithmetic and copies ran while one was open for 0% of the time, Pallas kernels for 17%

profile of v2, /device:TPU:1, one launch (start us, length us, event | category | flops | bytes accessed | tf_op | source)
XLA Modules:
  0.0 152.8 jit_solution(12769910118999213371)
XLA Ops:
  0.0 0.0 copy-start
  0.0 2.8 %shard_map.91 = (bf16[1024,128]{1,0:T(8,128)(2,1)S(1)}, bf16[2048,256]{1,0:T(8,128)(2,1)S(1)}, bf16[2048,512]{1,0:T(8,128)(2,1)S(1)}, s32[32]{0:T(128)S(1)}, s32[32]{0:T(128)S(1)}) custom-call(bf16[2048,256]{1,0:T(8,128)(2,1)} %bitcast.27, bf16[2048,512]{1,0:T(8,128)(2,1)} %bitcast.26, s32[16]{0:T(128)} %bitcast.30, s32[32]{0:T(128)} %bitcast.31), custom_call_target="tpu_custom_call" | custom-call | tf_op jit(solution)/shard_map/pallas_call | solution.py:41
  2.8 22.2 %all_to_all.30.x_ref = bf16[128,8,128]{2,1,0:T(8,128)(2,1)S(1)} all-to-all(bf16[128,8,128]{2,1,0:T(8,128)(2,1)S(1)} %bitcast.23), channel_id=1, replica_groups=mesh['front'=4,'rows_0'=4,'rows_1'=4,'rows_2'=2] {'front','rows_0','rows..., dimensions={0} | all-to-all | bytes 524288 | tf_op jit(solution)/shard_map/all_to_all | solution.py:358
  24.9 0.0 copy-done
  24.9 0.5 shard_map.92
  25.4 15.3 %all_to_all.31 = bf16[128,8,128]{2,1,0:T(8,128)(2,1)S(1)} all-to-all(bf16[128,8,128]{2,1,0:T(8,128)(2,1)S(1)} %shard_map.92), channel_id=1, replica_groups=mesh['front'=4,'rows_0'=4,'rows_1'=4,'rows_2'=2] {'front','rows_0','rows..., dimensions={0} | all-to-all | bytes 524288 | tf_op jit(solution)/shard_map/all_to_all | solution.py:358
  40.7 1.3 shard_map.93
  42.1 1.0 shard_map.95
  43.1 1.3 collective-permute-start.2
  44.4 1.0 shard_map.94
  45.4 0.2 collective-permute-start
  45.6 2.6 %collective-permute-start.1 = (bf16[1040,256]{1,0:T(8,128)(2,1)S(1)}, bf16[1040,256]{1,0:T(8,128)(2,1)S(1)}, u32[]{:S(2)}, u32[]{:S(2)}) collective-permute-start(bf16[1040,256]{1,0:T(8,128)(2,1)S(1)} %shard_map.95), channel_id=1, source_target_pairs={{0,96},{32,0},{64,32},{96,64},{1,97},{33,1},{65,33},{97,65},{2,98}... | collective-permute-start | bytes 1597448 | tf_op jit(solution)/shard_map/ppermute | solution.py:362
  48.2 1.0 shard_map.96.refs_0_.g0
  49.2 9.9 %shard_map.97 = (bf16[4096,512]{1,0:T(8,128)(2,1)S(1)}, bf16[4096,512]{1,0:T(8,128)(2,1)S(1)}) custom-call(s32[1]{0:T(128)} %get-tuple-element.26.refs_0_, s32[32]{0:T(128)S(1)} %get-tuple-element.19.refs_1_.t_ref, bf16[4096,512]{1,0:T(8,128)(2,1)} %bitcast.24, f32[512,512]{1,0:T(8,128)} %bitcast.28), custom_call_target="tpu_custom_call" | custom-call | tf_op jit(solution)/shard_map/pallas_call | solution.py:41
  59.1 0.5 shard_map.98.refs_1_
  59.6 0.0 collective-permute-done.2.refs_0_.g2
  59.6 0.5 shard_map.99.refs_2_
  60.1 10.0 %collective-permute-done.refs_0_.g1 = bf16[1040,256]{1,0:T(8,128)(2,1)S(1)} collective-permute-done((bf16[1040,256]{1,0:T(8,128)(2,1)S(1)}, bf16[1040,256]{1,0:T(8,128)(2,1)S(1)}, u32[]{:S(2)}, u32[]{:S(2)}) %collective-permute-start) | collective-permute-done | bytes 532512 | tf_op jit(solution)/shard_map/ppermute | solution.py:362
  70.1 0.0 collective-permute-done.1.refs_1_.g3
  70.1 0.7 shard_map.100
  70.9 13.0 %all_to_all.32.x_ref = bf16[32,8,512]{2,1,0:T(8,128)(2,1)S(1)} all-to-all(bf16[32,8,512]{2,1,0:T(8,128)(2,1)S(1)} %bitcast.21), channel_id=1, replica_groups=mesh['front'=4,'rows_0'=4,'rows_1'=4,'rows_2'=2] {'rows_0','rows_1','row..., dimensions={0} | all-to-all | bytes 524288 | tf_op jit(solution)/shard_map/all_to_all | solution.py:358
  83.8 0.1 shard_map.101
  83.9 12.4 %all_to_all.33 = bf16[32,8,512]{2,1,0:T(8,128)(2,1)S(1)} all-to-all(bf16[32,8,512]{2,1,0:T(8,128)(2,1)S(1)} %shard_map.101), channel_id=1, replica_groups=mesh['front'=4,'rows_0'=4,'rows_1'=4,'rows_2'=2] {'rows_0','rows_1','row..., dimensions={0} | all-to-all | bytes 524288 | tf_op jit(solution)/shard_map/all_to_all | solution.py:358
  96.3 1.4 shard_map.104
  97.7 0.7 collective-permute-start.5
  98.4 1.3 shard_map.102
  99.7 0.7 collective-permute-start.3
  100.4 1.3 shard_map.103
  101.7 2.3 %collective-permute-start.4 = (bf16[1040,256]{1,0:T(8,128)(2,1)S(1)}, bf16[1040,256]{1,0:T(8,128)(2,1)S(1)}, u32[]{:S(2)}, u32[]{:S(2)}) collective-permute-start(bf16[1040,256]{1,0:T(8,128)(2,1)S(1)} %shard_map.103), channel_id=1, source_target_pairs={{0,96},{32,0},{64,32},{96,64},{1,97},{33,1},{65,33},{97,65},{2,98}... | collective-permute-start | bytes 1597448 | tf_op jit(solution)/shard_map/ppermute | solution.py:362
  104.0 7.7 %shard_map.106 = (bf16[4096,512]{1,0:T(8,128)(2,1)S(1)}, bf16[4096,512]{1,0:T(8,128)(2,1)S(1)}) custom-call(s32[1]{0:T(128)} %get-tuple-element.30.refs_0_, bf16[4096,512]{1,0:T(8,128)(2,1)} %bitcast.25, f32[512,512]{1,0:T(8,128)} %bitcast.29), custom_call_target="tpu_custom_call" | custom-call | tf_op jit(solution)/shard_map/pallas_call | solution.py:41
  111.7 1.3 shard_map.105.refs_0_.g0
  113.0 0.5 shard_map.107.refs_1_
  113.5 0.0 collective-permute-done.5.refs_0_.g2
  113.5 0.5 shard_map.108.refs_2_
  114.0 10.8 %collective-permute-done.3.refs_0_.g1 = bf16[1040,256]{1,0:T(8,128)(2,1)S(1)} collective-permute-done((bf16[1040,256]{1,0:T(8,128)(2,1)S(1)}, bf16[1040,256]{1,0:T(8,128)(2,1)S(1)}, u32[]{:S(2)}, u32[]{:S(2)}) %collective-permute-start.3) | collective-permute-done | bytes 532512 | tf_op jit(solution)/shard_map/ppermute | solution.py:362
  124.7 0.0 collective-permute-done.4.refs_1_.g3
  124.7 0.7 shard_map.109
  125.5 12.6 %all_to_all.34.x_ref = bf16[32,8,512]{2,1,0:T(8,128)(2,1)S(1)} all-to-all(bf16[32,8,512]{2,1,0:T(8,128)(2,1)S(1)} %bitcast.22), channel_id=1, replica_groups=mesh['front'=4,'rows_0'=4,'rows_1'=4,'rows_2'=2] {'rows_0','rows_1','row..., dimensions={0} | all-to-all | bytes 524288 | tf_op jit(solution)/shard_map/all_to_all | solution.py:358
  138.1 0.1 shard_map.110
  138.1 12.4 %all_to_all.35 = bf16[32,8,512]{2,1,0:T(8,128)(2,1)S(1)} all-to-all(bf16[32,8,512]{2,1,0:T(8,128)(2,1)S(1)} %shard_map.110), channel_id=1, replica_groups=mesh['front'=4,'rows_0'=4,'rows_1'=4,'rows_2'=2] {'rows_0','rows_1','row..., dimensions={0} | all-to-all | bytes 524288 | tf_op jit(solution)/shard_map/all_to_all | solution.py:358
  150.6 2.1 %shard_map.111 = bf16[4096,256]{1,0:T(8,128)(2,1)} custom-call(bf16[256,512]{1,0:T(8,128)(2,1)S(1)} %bitcast.19, bf16[1040,256]{1,0:T(8,128)(2,1)S(1)} %shard_map.105.refs_0_.g0, bf16[1040,256]{1,0:T(8,128)(2,1)S(1)} %collective-permute-done.3.refs_0_.g1, bf16[1040,256]{1,0:T(8,128)(2,1)S(1)} %collective-permute-done.5.refs_0_.g2, ...), custom_call_target="tpu_custom_call" | custom-call | tf_op jit(solution)/shard_map/pallas_call | solution.py:41
Async XLA Ops:
  0.0 24.9 %copy-start = (f32[512,512]{1,0:T(8,128)S(1)}, f32[512,512]{1,0:T(8,128)}, u32[]{:S(2)}) copy-start(f32[512,512]{1,0:T(8,128)} %t_ref.1) | copy-start | bytes 3145732
  43.1 16.5 %collective-permute-start.2 = (bf16[1040,256]{1,0:T(8,128)(2,1)S(1)}, bf16[1040,256]{1,0:T(8,128)(2,1)S(1)}, u32[]{:S(2)}, u32[]{:S(2)}) collective-permute-start(bf16[1040,256]{1,0:T(8,128)(2,1)S(1)} %get-tuple-element.25), channel_id=1, source_target_pairs={{0,64},{32,96},{64,0},{96,32},{1,65},{33,97},{65,1},{97,33},{2,66}... | collective-permute-start | bytes 1597448 | tf_op jit(solution)/shard_map/ppermute | solution.py:362
  45.4 24.7 %collective-permute-start = (bf16[1040,256]{1,0:T(8,128)(2,1)S(1)}, bf16[1040,256]{1,0:T(8,128)(2,1)S(1)}, u32[]{:S(2)}, u32[]{:S(2)}) collective-permute-start(bf16[1040,256]{1,0:T(8,128)(2,1)S(1)} %shard_map.94), channel_id=1, source_target_pairs={{0,32},{32,64},{64,96},{96,0},{1,33},{33,65},{65,97},{97,1},{2,34}... | collective-permute-start | bytes 1597448 | tf_op jit(solution)/shard_map/ppermute | solution.py:362
  45.6 24.5 %collective-permute-start.1 = (bf16[1040,256]{1,0:T(8,128)(2,1)S(1)}, bf16[1040,256]{1,0:T(8,128)(2,1)S(1)}, u32[]{:S(2)}, u32[]{:S(2)}) collective-permute-start(bf16[1040,256]{1,0:T(8,128)(2,1)S(1)} %shard_map.95), channel_id=1, source_target_pairs={{0,96},{32,0},{64,32},{96,64},{1,97},{33,1},{65,33},{97,65},{2,98}... | collective-permute-start | bytes 1597448 | tf_op jit(solution)/shard_map/ppermute | solution.py:362
  97.7 15.8 %collective-permute-start.5 = (bf16[1040,256]{1,0:T(8,128)(2,1)S(1)}, bf16[1040,256]{1,0:T(8,128)(2,1)S(1)}, u32[]{:S(2)}, u32[]{:S(2)}) collective-permute-start(bf16[1040,256]{1,0:T(8,128)(2,1)S(1)} %get-tuple-element.29), channel_id=1, source_target_pairs={{0,64},{32,96},{64,0},{96,32},{1,65},{33,97},{65,1},{97,33},{2,66}... | collective-permute-start | bytes 1597448 | tf_op jit(solution)/shard_map/ppermute | solution.py:362
  99.7 25.0 %collective-permute-start.3 = (bf16[1040,256]{1,0:T(8,128)(2,1)S(1)}, bf16[1040,256]{1,0:T(8,128)(2,1)S(1)}, u32[]{:S(2)}, u32[]{:S(2)}) collective-permute-start(bf16[1040,256]{1,0:T(8,128)(2,1)S(1)} %shard_map.102), channel_id=1, source_target_pairs={{0,32},{32,64},{64,96},{96,0},{1,33},{33,65},{65,97},{97,1},{2,34}... | collective-permute-start | bytes 1597448 | tf_op jit(solution)/shard_map/ppermute | solution.py:362
  101.7 23.0 %collective-permute-start.4 = (bf16[1040,256]{1,0:T(8,128)(2,1)S(1)}, bf16[1040,256]{1,0:T(8,128)(2,1)S(1)}, u32[]{:S(2)}, u32[]{:S(2)}) collective-permute-start(bf16[1040,256]{1,0:T(8,128)(2,1)S(1)} %shard_map.103), channel_id=1, source_target_pairs={{0,96},{32,0},{64,32},{96,64},{1,97},{33,1},{65,33},{97,65},{2,98}... | collective-permute-start | bytes 1597448 | tf_op jit(solution)/shard_map/ppermute | solution.py:362
